TPU v7x, 32 devices: a whole 2x2x4 slice. The times are simulated.
32 devices in a mesh: chain: 2 (over y), cell: 4 (over z), col: 4 (over x, core).
Axes of the slice: x: 2, y: 2, z: 4, core: 2. Of those that a mesh axis runs over, the one named last changes fastest.
Arguments:
- grad: float32 [16384, 64], P(('chain', 'cell', 'col')), parts along dimension 0, may hold values from -6 to 6
- near_tiles: bfloat16 [4, 2, 2048, 2048], P('cell', None, 'col'), may hold values from -0.09375 to 0.09375
- tile_count: int32 [4], replicated, may hold values from 1 to 2
- near_offset: int32 [4], replicated, may hold values from -2 to 2, as said below
- far_src: int32 [4, 8], replicated, may hold values from 0 to 3
- far_count: int32 [4], replicated, may hold values from 1 to 8
- far_cores: float32 [4, 8, 64, 64], P('cell'), may hold values from -0.25 to 0.25
- basis_out: bfloat16 [8192, 64], P(('cell', 'col')), may hold values from -0.75 to 0.75
- basis_in: bfloat16 [8192, 64], P(('cell', 'col')), may hold values from -0.125 to 0.125
Outputs:
- step_block: float32 [16384, 64], P(('chain', 'cell', 'col')), parts along dimension 0
There are 2 independent parts, one for each index of `chain`. A program takes and returns all parts, laid end to end along the dimension named above; an argument that names none is the same for every part. Nothing has to cross between parts.
Inputs may be any that keep to these rules, and one draw needn't show every extreme that they name: c + near_offset[c] is a cluster of the chain, and near_offset[c] is never 0.
All inputs are finite; a program needn't handle non-finite values.
Results may differ from a plain program's by a relative error of at most 0.0035.
Values may be sent and summed in bfloat16 or wider, within the bound.
No kernel may reach another device: no remote copies, remote signals or barrier semaphores. Data moves between devices by JAX's collectives and lax.ppermute only.
A program may use at most 64 MiB of HBM per device.

v0:
```python
import jax
import jax.numpy as jnp
from jax import lax
from jax.sharding import PartitionSpec as P


def shifted(value, axis, by):
    devices = lax.axis_size(axis)
    pairs = [(i, i + by) for i in range(devices) if 0 <= i + by < devices]
    return lax.ppermute(value, axis, pairs)


def pick_offset(stacked, offset):
    position = offset + 2 - (offset > 0).astype(jnp.int32)
    return lax.dynamic_index_in_dim(stacked, position, 0, keepdims=False)


def coupling(table, sources, count, cores):
    picked = jnp.take(table, sources, axis=0)
    slots = jnp.arange(cores.shape[0], dtype=jnp.int32)
    masked = jnp.where((slots < count)[:, None, None], cores, jnp.zeros_like(cores))
    return jnp.einsum("kab,kbw->aw", masked, picked, precision=lax.Precision.HIGHEST)


def body(
    grad, near_tiles, tile_count, near_offset, far_src, far_count, far_cores, basis_out, basis_in
):
    owner = lax.axis_index("cell")
    rounded = grad.astype(jnp.bfloat16)
    offset = near_offset[owner]
    steps_list = (-2, -1, 1, 2)
    whole = lax.all_gather(rounded, "col", axis=0, tiled=True)
    moved = [shifted(whole, "cell", -step) for step in steps_list]
    beside = pick_offset(jnp.stack(moved), offset)
    tiles = near_tiles[0]
    own_term = jnp.dot(tiles[0], whole, preferred_element_type=jnp.float32)
    other_term = jnp.dot(tiles[1], beside, preferred_element_type=jnp.float32)
    near = own_term + jnp.where(tile_count[owner] == 2, other_term, jnp.zeros_like(other_term))
    partial_proj = lax.dot_general(
        basis_in, rounded, (((0,), (0,)), ((), ())), preferred_element_type=jnp.float32
    )
    sources = far_src[owner]
    count = far_count[owner]
    cores = far_cores[0]
    proj = lax.psum(partial_proj, "col")
    table = lax.all_gather(proj[None], "cell", axis=0, tiled=True)
    core_block = coupling(table, sources, count, cores).astype(jnp.bfloat16)
    far = jnp.dot(basis_out, core_block, preferred_element_type=jnp.float32)
    return near + far


def solution(mesh):
    placed = (
        P(("chain", "cell", "col"), None),
        P("cell", None, "col", None),
        P(),
        P(),
        P(),
        P(),
        P("cell", None, None, None),
        P(("cell", "col"), None),
        P(("cell", "col"), None),
    )
    return jax.shard_map(
        body,
        mesh=mesh,
        in_specs=placed,
        out_specs=P(("chain", "cell", "col"), None),
        check_vma=False,
    )
```

profile of v0, /device:TPU:0, one launch (start us, length us, event | category | flops | bytes accessed | tf_op | source)
XLA Modules:
  0.0 60.8 jit_solution(2780922674257491303)
XLA Ops:
  0.0 0.0 copy-start
  0.0 0.9 %convert_element_type.10 = bf16[512,64]{0,1:T(8,128)(2,1)S(1)} convert(f32[512,64]{0,1:T(8,128)} %param.9) | non-fusion elementwise | flops 32768 | bytes 196608 | tf_op jit(solution)/shard_map/convert_element_type | solution.py:29
  1.0 7.2 %all_gather.6 = bf16[2048,64]{0,1:T(8,128)(2,1)S(1)} all-gather(bf16[512,64]{0,1:T(8,128)(2,1)S(1)} %convert_element_type.10), channel_id=1, replica_groups=mesh['chain'=2,'cell'=4,'col'=4] {'col'}, dimensions={0}, use_global_device_ids=true | all-gather | bytes 327680 | tf_op jit(solution)/shard_map/all_gather | solution.py:32
  8.2 4.5 %collective-permute-start = (bf16[2048,64]{0,1:T(8,128)(2,1)S(1)}, bf16[2048,64]{0,1:T(8,128)(2,1)S(1)}, u32[]{:S(2)}, u32[]{:S(2)}) collective-permute-start(bf16[2048,64]{0,1:T(8,128)(2,1)S(1)} %all_gather.6), channel_id=1, source_target_pairs={{0,8},{4,12},{1,9},{5,13},{2,10},{6,14},{3,11},{7,15},{16,24},{20,... | collective-permute-start | bytes 786440 | tf_op jit(solution)/shard_map/ppermute | solution.py:10
  12.7 3.5 %collective-permute-start.1 = (bf16[2048,64]{0,1:T(8,128)(2,1)S(1)}, bf16[2048,64]{0,1:T(8,128)(2,1)S(1)}, u32[]{:S(2)}, u32[]{:S(2)}) collective-permute-start(bf16[2048,64]{0,1:T(8,128)(2,1)S(1)} %all_gather.6), channel_id=1, source_target_pairs={{0,4},{4,8},{8,12},{1,5},{5,9},{9,13},{2,6},{6,10},{10,14},{3,7},{... | collective-permute-start | bytes 786440 | tf_op jit(solution)/shard_map/ppermute | solution.py:10
  16.2 1.3 %collective-permute-start.2 = (bf16[2048,64]{0,1:T(8,128)(2,1)S(1)}, bf16[2048,64]{0,1:T(8,128)(2,1)S(1)}, u32[]{:S(2)}, u32[]{:S(2)}) collective-permute-start(bf16[2048,64]{0,1:T(8,128)(2,1)S(1)} %all_gather.6), channel_id=1, source_target_pairs={{4,0},{8,4},{12,8},{5,1},{9,5},{13,9},{6,2},{10,6},{14,10},{7,3},{... | collective-permute-start | bytes 786440 | tf_op jit(solution)/shard_map/ppermute | solution.py:10
  17.5 1.3 %collective-permute-start.3 = (bf16[2048,64]{0,1:T(8,128)(2,1)S(1)}, bf16[2048,64]{0,1:T(8,128)(2,1)S(1)}, u32[]{:S(2)}, u32[]{:S(2)}) collective-permute-start(bf16[2048,64]{0,1:T(8,128)(2,1)S(1)} %all_gather.6), channel_id=1, source_target_pairs={{8,0},{12,4},{9,1},{13,5},{10,2},{14,6},{11,3},{15,7},{24,16},{28,... | collective-permute-start | bytes 786440 | tf_op jit(solution)/shard_map/ppermute | solution.py:10
  18.8 1.2 %dynamic_slice.19 = s32[1]{0:T(128)} dynamic-slice(s32[4]{0:T(128)} %param.14, s32[]{:T(128)S(6)} %select_n.45), dynamic_slice_sizes={1} | dynamic-slice | bytes 12 | tf_op jit(solution)/shard_map/dynamic_slice | solution.py:43
  20.1 0.7 %fusion.30 = s32[8]{0:T(128)S(1)} fusion(s32[4,8]{1,0:T(4,128)} %param.13, s32[]{:T(128)S(6)} %select_n.45), kind=kLoop, calls=%fused_computation.35 | loop fusion | flops 24 | bytes 68 | tf_op jit(solution)/shard_map/jit(_take)/jit(_where)/select_n | solution.py:19
  20.8 1.3 %compare_and_fusion = (pred[8]{0:T(512)(128)(4,1)S(1)}, pred[8]{0:T(512)(128)(4,1)S(1)}) fusion(s32[4,8]{1,0:T(4,128)} %param.13, s32[]{:T(128)S(6)} %select_n.45, s32[]{:T(128)} %bitcast.10), kind=kLoop, calls=%fused_computation.32 | loop fusion | flops 56 | bytes 56 | tf_op jit(solution)/shard_map/jit(_take)/and | solution.py:19
  22.1 1.0 %convolution_bitcast_fusion.1 = f32[1,64,64]{2,1,0:T(8,128)S(1)} fusion(bf16[512,64]{0,1:T(8,128)(2,1)} %param.17, bf16[512,64]{0,1:T(8,128)(2,1)S(1)} %convert_element_type.10), kind=kOutput, calls=%fused_computation.12 | convolution fusion | flops 4194304 | bytes 147456 | tf_op jit(solution)/shard_map/dot_general | solution.py:39
  23.1 11.4 %psum.7 = f32[1,64,64]{2,1,0:T(8,128)S(1)} all-reduce(f32[1,64,64]{2,1,0:T(8,128)S(1)} %convolution_bitcast_fusion.1), channel_id=1, replica_groups=mesh['chain'=2,'cell'=4,'col'=4] {'col'}, use_global_device_ids=true, to_apply=%region_0.1 | all-reduce | flops 4096 | bytes 32768 | tf_op jit(solution)/shard_map/psum | solution.py:45
  34.5 14.3 %all_gather.7 = f32[4,64,64]{2,1,0:T(8,128)S(1)} all-gather(f32[1,64,64]{2,1,0:T(8,128)S(1)} %psum.7), channel_id=1, replica_groups=mesh['chain'=2,'cell'=4,'col'=4] {'cell'}, dimensions={0}, use_global_device_ids=true | all-gather | bytes 81920 | tf_op jit(solution)/shard_map/all_gather | solution.py:46
  48.8 0.6 gather_fusion
  49.3 1.4 %fusion.18 = bf16[64,64]{1,0:T(8,128)(2,1)S(1)} fusion(f32[1,8,64,64]{3,2,1,0:T(8,128)} %param.15, f32[8,64,64]{2,1,0:T(8,128)S(1)} %gather_fusion, pred[8]{0:T(512)(128)(4,1)S(1)} %get-tuple-element.5, pred[8]{0:T(512)(128)(4,1)S(1)} %get-tuple-element.6), kind=kOutput, calls=%fused_computation.14 | convolution fusion | flops 25235456 | bytes 270352 | tf_op jit(solution)/shard_map/kab,kbw->aw/dot_general | solution.py:22
  50.8 1.2 %dynamic_slice.17 = s32[1]{0:T(128)} dynamic-slice(s32[4]{0:T(128)} %param.12, s32[]{:T(128)S(6)} %select_n.45), dynamic_slice_sizes={1} | dynamic-slice | bytes 12 | tf_op jit(solution)/shard_map/dynamic_slice | solution.py:30
  53.3 1.3 %dynamic_slice.16 = s32[1]{0:T(128)} dynamic-slice(s32[4]{0:T(128)} %param.11, s32[]{:T(128)S(6)} %select_n.45), dynamic_slice_sizes={1} | dynamic-slice | bytes 12 | tf_op jit(solution)/shard_map/dynamic_slice | solution.py:38
  55.2 0.0 copy-done
  55.2 0.2 convolution_bitcast_fusion
  55.4 0.0 collective-permute-done
  55.4 0.0 collective-permute-done.1
  55.4 0.0 collective-permute-done.2
  55.4 0.0 collective-permute-done.3
  55.4 2.4 %fusion.15 = f32[512,64]{0,1:T(8,128)S(1)} fusion(bf16[1,2,512,2048]{3,2,1,0:T(8,128)(2,1)} %param.10, s32[]{:T(128)S(6)} %select_n.47, bf16[1,2048,64]{1,2,0:T(8,128)(2,1)S(1)} %bitcast.48, bf16[1,2048,64]{1,2,0:T(8,128)(2,1)S(1)} %bitcast.49, bf16[1,2048,64]{1,2,0:T(8,128)(2,1)S(1)} %bitcast.50, bf16[1,2048,64]{1,2,0:T(8,128)(2,1)S(1)} %bitcast.51, ...), kind=kOutput, calls=%fused_computation.10 | convolution fusion | flops 134643712 | bytes 3277316 | tf_op jit(solution)/shard_map/dot_general | solution.py:37
  57.8 3.0 %fusion.9 = f32[512,64]{0,1:T(8,128)} fusion(f32[512,64]{0,1:T(8,128)S(1)} %convolution_bitcast_fusion, f32[512,64]{0,1:T(8,128)S(1)} %fusion.15, bf16[2048,64]{0,1:T(8,128)(2,1)S(1)} %all_gather.6, bf16[1,2,512,2048]{3,2,1,0:T(8,128)(2,1)} %param.10), kind=kOutput, calls=%fused_computation.8 | convolution fusion | flops 134283264 | bytes 2752512 | tf_op jit(solution)/shard_map/dot_general | solution.py:36
  (1 shorter events, 0.0 us)
Async XLA Ops:
  0.0 55.2 %copy-start = (bf16[512,64]{0,1:T(8,128)(2,1)S(1)}, bf16[512,64]{0,1:T(8,128)(2,1)}, u32[]{:S(2)}) copy-start(bf16[512,64]{0,1:T(8,128)(2,1)} %param.16) | copy-start | bytes 196612
  8.2 47.2 %collective-permute-start = (bf16[2048,64]{0,1:T(8,128)(2,1)S(1)}, bf16[2048,64]{0,1:T(8,128)(2,1)S(1)}, u32[]{:S(2)}, u32[]{:S(2)}) collective-permute-start(bf16[2048,64]{0,1:T(8,128)(2,1)S(1)} %all_gather.6), channel_id=1, source_target_pairs={{0,8},{4,12},{1,9},{5,13},{2,10},{6,14},{3,11},{7,15},{16,24},{20,... | collective-permute-start | bytes 786440 | tf_op jit(solution)/shard_map/ppermute | solution.py:10
  12.7 42.7 %collective-permute-start.1 = (bf16[2048,64]{0,1:T(8,128)(2,1)S(1)}, bf16[2048,64]{0,1:T(8,128)(2,1)S(1)}, u32[]{:S(2)}, u32[]{:S(2)}) collective-permute-start(bf16[2048,64]{0,1:T(8,128)(2,1)S(1)} %all_gather.6), channel_id=1, source_target_pairs={{0,4},{4,8},{8,12},{1,5},{5,9},{9,13},{2,6},{6,10},{10,14},{3,7},{... | collective-permute-start | bytes 786440 | tf_op jit(solution)/shard_map/ppermute | solution.py:10
  16.2 39.2 %collective-permute-start.2 = (bf16[2048,64]{0,1:T(8,128)(2,1)S(1)}, bf16[2048,64]{0,1:T(8,128)(2,1)S(1)}, u32[]{:S(2)}, u32[]{:S(2)}) collective-permute-start(bf16[2048,64]{0,1:T(8,128)(2,1)S(1)} %all_gather.6), channel_id=1, source_target_pairs={{4,0},{8,4},{12,8},{5,1},{9,5},{13,9},{6,2},{10,6},{14,10},{7,3},{... | collective-permute-start | bytes 786440 | tf_op jit(solution)/shard_map/ppermute | solution.py:10
  17.5 37.9 %collective-permute-start.3 = (bf16[2048,64]{0,1:T(8,128)(2,1)S(1)}, bf16[2048,64]{0,1:T(8,128)(2,1)S(1)}, u32[]{:S(2)}, u32[]{:S(2)}) collective-permute-start(bf16[2048,64]{0,1:T(8,128)(2,1)S(1)} %all_gather.6), channel_id=1, source_target_pairs={{8,0},{12,4},{9,1},{13,5},{10,2},{14,6},{11,3},{15,7},{24,16},{28,... | collective-permute-start | bytes 786440 | tf_op jit(solution)/shard_map/ppermute | solution.py:10
where the time goes:
time: 61.3 us; the launch traced here: 60.8 us
  blocking collectives  32.9 us (54%)
  starting transfers between devices  10.6 us (17%)
  matrix products  7.95 us (13%)
  local copies, waits for them, and re-layouts  4.33 us (7%)
  other arithmetic  2.98 us (5%)
  between operations  2.04 us (3%)
    all_gather x1, blocking collectives, body(): table = lax.all_gather(proj[None], 'cell', axis=0, tiled=True)  14.3 us
    psum x1, blocking collectives, body(): proj = lax.psum(partial_proj, 'col')  11.4 us
    ppermute x4, starting transfers between devices, shifted(): return lax.ppermute(value, axis, pairs)  10.6 us
    all_gather x1, blocking collectives, body(): whole = lax.all_gather(rounded, 'col', axis=0, tiled=True)  7.22 us
    dot_general x1, matrix products, body(): own_term = jnp.dot(tiles[0], whole, preferred_element_type=jnp.float32)  3.01 us
    dot_general x1, matrix products, body(): other_term = jnp.dot(tiles[1], beside, preferred_element_type=jnp.float32)  2.36 us
    dot_general x1, matrix products, coupling(): jnp.einsum('kab,kbw->aw', masked, picked, precision=lax.Precision.HIGHEST)  1.42 us
    and x1, other arithmetic, coupling(): picked = jnp.take(table, sources, axis=0)  1.34 us
  transfers between devices with their start and end apart: 4, of which 0 were waited for; matrix products, arithmetic and copies ran while one was open for 15% of the time, Pallas kernels for 0%

commit v1 on v0

--- a/solution.py
+++ b/solution.py
@@ -2,6 +2,12 @@
 import jax.numpy as jnp
 from jax import lax
 from jax.sharding import PartitionSpec as P
+
+
+def time_the_weights(xs, d_out):
+    return jnp.concatenate(
+        lax.all_to_all(jnp.stack(lax.axis_size("cell") * [xs]), "cell", 0, 0), axis=d_out
+    )
 
 
 def shifted(value, axis, by):
@@ -43,7 +49,7 @@
     count = far_count[owner]
     cores = far_cores[0]
     proj = lax.psum(partial_proj, "col")
-    table = lax.all_gather(proj[None], "cell", axis=0, tiled=True)
+    table = time_the_weights(proj[None], 0)
     core_block = coupling(table, sources, count, cores).astype(jnp.bfloat16)
     far = jnp.dot(basis_out, core_block, preferred_element_type=jnp.float32)
     return near + far

time: 61.3 us -> 53.7 us (0.88)
  blocking collectives: 32.9 us -> 18.6 us
  starting transfers between devices: 10.6 us -> 16.7 us
  matrix products: 7.95 us -> 6.52 us
  local copies, waits for them, and re-layouts: 4.33 us -> 5.72 us
  other arithmetic: 2.98 us -> 3.71 us
    all_gather x1 -> x0, blocking collectives: 14.3 us -> none  [body(): table = lax.all_gather(proj[None], 'cell', axis=0, tiled=True)]
    all_to_all x0 -> x1, starting transfers between devices: none -> 6.13 us  [time_the_weights(): lax.all_to_all(jnp.stack(lax.axis_size('cell') * [xs]), 'cell', 0, 0)]
    dot_general x1, matrix products: 3.01 us -> 1.44 us  [body(): own_term = jnp.dot(tiles[0], whole, preferred_element_type=jnp.float32)]
    unnamed x2 -> x6, local copies, waits for them, and re-layouts: 0.01 us -> 0.89 us
    all_to_all x0 -> x1, other arithmetic: none -> 0.81 us  [time_the_weights(): lax.all_to_all(jnp.stack(lax.axis_size('cell') * [xs]), 'cell', 0, 0)]
  transfers between devices with their start and end apart: 4 -> 5, of which waited for: 0 -> 0; matrix products, arithmetic and copies ran while one was open for 15% -> 21% of each run, Pallas kernels for 0% -> 0%
where the time goes in v1:
time: 53.7 us; the launch traced here: 53.2 us
  blocking collectives  18.6 us (35%)
  starting transfers between devices  16.7 us (31%)
  matrix products  6.52 us (12%)
  local copies, waits for them, and re-layouts  5.72 us (11%)
  other arithmetic  3.71 us (7%)
  between operations  1.93 us (4%)
    psum x1, blocking collectives, body(): proj = lax.psum(partial_proj, 'col')  11.4 us
    ppermute x4, starting transfers between devices, shifted(): return lax.ppermute(value, axis, pairs)  10.6 us
    all_gather x1, blocking collectives, body(): whole = lax.all_gather(rounded, 'col', axis=0, tiled=True)  7.22 us
    all_to_all x1, starting transfers between devices, time_the_weights(): lax.all_to_all(jnp.stack(lax.axis_size('cell') * [xs]), 'cell', 0, 0)  6.13 us
    dot_general x1, matrix products, body(): other_term = jnp.dot(tiles[1], beside, preferred_element_type=jnp.float32)  2.36 us
    dot_general x1, matrix products, coupling(): jnp.einsum('kab,kbw->aw', masked, picked, precision=lax.Precision.HIGHEST)  1.57 us
    dot_general x1, matrix products, body(): own_term = jnp.dot(tiles[0], whole, preferred_element_type=jnp.float32)  1.44 us
    dynamic_slice x1, local copies, waits for them, and re-layouts, body(): offset = near_offset[owner]  1.27 us
  transfers between devices with their start and end apart: 5, of which 0 were waited for; matrix products, arithmetic and copies ran while one was open for 21% of the time, Pallas kernels for 0%

profile of v1, /device:TPU:0, one launch (start us, length us, event | category | flops | bytes accessed | tf_op | source)
XLA Modules:
  0.0 53.2 jit_solution(8446998134752604842)
XLA Ops:
  0.0 0.0 copy-start
  0.0 0.9 %convert_element_type.10 = bf16[512,64]{0,1:T(8,128)(2,1)S(1)} convert(f32[512,64]{0,1:T(8,128)} %param.9) | non-fusion elementwise | flops 32768 | bytes 196608 | tf_op jit(solution)/shard_map/convert_element_type | solution.py:35
  1.0 7.2 %all_gather.3 = bf16[2048,64]{0,1:T(8,128)(2,1)S(1)} all-gather(bf16[512,64]{0,1:T(8,128)(2,1)S(1)} %convert_element_type.10), channel_id=1, replica_groups=mesh['chain'=2,'cell'=4,'col'=4] {'col'}, dimensions={0}, use_global_device_ids=true | all-gather | bytes 327680 | tf_op jit(solution)/shard_map/all_gather | solution.py:38
  8.2 4.5 %collective-permute-start = (bf16[2048,64]{0,1:T(8,128)(2,1)S(1)}, bf16[2048,64]{0,1:T(8,128)(2,1)S(1)}, u32[]{:S(2)}, u32[]{:S(2)}) collective-permute-start(bf16[2048,64]{0,1:T(8,128)(2,1)S(1)} %all_gather.3), channel_id=1, source_target_pairs={{0,8},{4,12},{1,9},{5,13},{2,10},{6,14},{3,11},{7,15},{16,24},{20,... | collective-permute-start | bytes 786440 | tf_op jit(solution)/shard_map/ppermute | solution.py:16
  12.7 3.5 %collective-permute-start.1 = (bf16[2048,64]{0,1:T(8,128)(2,1)S(1)}, bf16[2048,64]{0,1:T(8,128)(2,1)S(1)}, u32[]{:S(2)}, u32[]{:S(2)}) collective-permute-start(bf16[2048,64]{0,1:T(8,128)(2,1)S(1)} %all_gather.3), channel_id=1, source_target_pairs={{0,4},{4,8},{8,12},{1,5},{5,9},{9,13},{2,6},{6,10},{10,14},{3,7},{... | collective-permute-start | bytes 786440 | tf_op jit(solution)/shard_map/ppermute | solution.py:16
  16.2 1.3 %collective-permute-start.2 = (bf16[2048,64]{0,1:T(8,128)(2,1)S(1)}, bf16[2048,64]{0,1:T(8,128)(2,1)S(1)}, u32[]{:S(2)}, u32[]{:S(2)}) collective-permute-start(bf16[2048,64]{0,1:T(8,128)(2,1)S(1)} %all_gather.3), channel_id=1, source_target_pairs={{4,0},{8,4},{12,8},{5,1},{9,5},{13,9},{6,2},{10,6},{14,10},{7,3},{... | collective-permute-start | bytes 786440 | tf_op jit(solution)/shard_map/ppermute | solution.py:16
  17.5 1.3 %collective-permute-start.3 = (bf16[2048,64]{0,1:T(8,128)(2,1)S(1)}, bf16[2048,64]{0,1:T(8,128)(2,1)S(1)}, u32[]{:S(2)}, u32[]{:S(2)}) collective-permute-start(bf16[2048,64]{0,1:T(8,128)(2,1)S(1)} %all_gather.3), channel_id=1, source_target_pairs={{8,0},{12,4},{9,1},{13,5},{10,2},{14,6},{11,3},{15,7},{24,16},{28,... | collective-permute-start | bytes 786440 | tf_op jit(solution)/shard_map/ppermute | solution.py:16
  18.8 1.0 %fusion.34 = f32[64,64]{1,0:T(8,128)S(1)} fusion(bf16[512,64]{0,1:T(8,128)(2,1)} %param.17, bf16[512,64]{0,1:T(8,128)(2,1)S(1)} %convert_element_type.10), kind=kOutput, calls=%fused_computation.39 | convolution fusion | flops 4194304 | bytes 147456 | tf_op jit(solution)/shard_map/dot_general | solution.py:45
  19.8 11.4 %psum.7 = f32[64,64]{1,0:T(8,128)S(1)} all-reduce(f32[64,64]{1,0:T(8,128)S(1)} %fusion.34), channel_id=1, replica_groups=mesh['chain'=2,'cell'=4,'col'=4] {'col'}, use_global_device_ids=true, to_apply=%region_0.1 | all-reduce | flops 4096 | bytes 32768 | tf_op jit(solution)/shard_map/psum | solution.py:51
  31.2 0.8 %reshape.65 = f32[4,1,4096]{2,1,0:T(1,128)} reshape(f32[4,1,64,64]{3,2,1,0:T(8,128)S(1)} %stack.23) | data formatting | bytes 131072
  32.0 6.1 %all-to-all-start = ((f32[4,1,4096]{2,1,0:T(1,128)}), f32[4,1,4096]{2,1,0:T(1,128)S(1)}, u32[]{:S(2)}, u32[]{:S(2)}) async-start(f32[4,1,4096]{2,1,0:T(1,128)} %reshape.65), calls=%async_computation | async-start | bytes 131072 | tf_op jit(solution)/shard_map/all_to_all | solution.py:9
  38.1 1.3 %dynamic_slice.17 = s32[1]{0:T(128)} dynamic-slice(s32[4]{0:T(128)} %param.12, s32[]{:T(128)S(6)} %select_n.45), dynamic_slice_sizes={1} | dynamic-slice | bytes 12 | tf_op jit(solution)/shard_map/dynamic_slice | solution.py:36
  40.6 1.2 %dynamic_slice.16 = s32[1]{0:T(128)} dynamic-slice(s32[4]{0:T(128)} %param.11, s32[]{:T(128)S(6)} %select_n.45), dynamic_slice_sizes={1} | dynamic-slice | bytes 12 | tf_op jit(solution)/shard_map/dynamic_slice | solution.py:44
  42.4 1.2 %dynamic_slice.19 = s32[1]{0:T(128)} dynamic-slice(s32[4]{0:T(128)} %param.14, s32[]{:T(128)S(6)} %select_n.45), dynamic_slice_sizes={1} | dynamic-slice | bytes 12 | tf_op jit(solution)/shard_map/dynamic_slice | solution.py:49
  43.6 0.7 %fusion.30 = s32[8]{0:T(128)S(1)} fusion(s32[4,8]{1,0:T(4,128)} %param.13, s32[]{:T(128)S(6)} %select_n.45), kind=kLoop, calls=%fused_computation.34 | loop fusion | flops 24 | bytes 68 | tf_op jit(solution)/shard_map/jit(_take)/jit(_where)/select_n | solution.py:25
  44.3 1.3 %compare_and_fusion = (pred[8]{0:T(512)(128)(4,1)S(1)}, pred[8]{0:T(512)(128)(4,1)S(1)}) fusion(s32[4,8]{1,0:T(4,128)} %param.13, s32[]{:T(128)S(6)} %select_n.45, s32[]{:T(128)} %bitcast.10), kind=kLoop, calls=%fused_computation.31 | loop fusion | flops 56 | bytes 56 | tf_op jit(solution)/shard_map/jit(_take)/and | solution.py:25
  45.6 0.0 all-to-all-done
  45.6 0.5 broadcast.46
  46.1 0.8 %reduce = f32[4,4096]{1,0:T(4,128)S(1)} reduce(f32[4,1,4096]{2,1,0:T(1,128)S(1)} %all-to-all-done, f32[]{:T(128)} %broadcast.46), dimensions={1}, to_apply=%all_to_all.3.reduce_sub_computation | reduce | bytes 131076 | tf_op jit(solution)/shard_map/all_to_all | solution.py:9
  46.9 0.1 reshape.66
  47.0 0.6 %gather_fusion = f32[8,64,64]{2,1,0:T(8,128)S(1)} fusion(f32[4,64,64]{2,1,0:T(8,128)S(1)} %bitcast.47, s32[1024]{0:T(1024)S(1)} %pad_clamp_fusion), kind=kCustom, calls=%fused_computation | custom fusion | bytes 262176 | tf_op jit(solution)/shard_map/jit(_take)/gather | solution.py:25
  47.6 0.0 copy-start.1
  47.6 1.6 %fusion.18 = bf16[64,64]{1,0:T(8,128)(2,1)S(1)} fusion(f32[1,8,64,64]{3,2,1,0:T(8,128)} %param.15, f32[8,64,64]{2,1,0:T(8,128)S(1)} %gather_fusion, pred[8]{0:T(512)(128)(4,1)S(1)} %get-tuple-element.5, pred[8]{0:T(512)(128)(4,1)S(1)} %get-tuple-element.6), kind=kOutput, calls=%fused_computation.13 | convolution fusion | flops 25235456 | bytes 270352 | tf_op jit(solution)/shard_map/kab,kbw->aw/dot_general | solution.py:28
  49.2 0.0 copy-done
  49.2 0.2 convolution_bitcast_fusion
  49.4 0.0 collective-permute-done
  49.4 0.0 collective-permute-done.1
  49.4 0.0 collective-permute-done.2
  49.4 0.0 collective-permute-done.3
  49.4 2.4 %fusion.15 = f32[512,64]{0,1:T(8,128)S(1)} fusion(bf16[1,2,512,2048]{3,2,1,0:T(8,128)(2,1)} %param.10, s32[]{:T(128)S(6)} %select_n.47, bf16[1,2048,64]{1,2,0:T(8,128)(2,1)S(1)} %bitcast.48, bf16[1,2048,64]{1,2,0:T(8,128)(2,1)S(1)} %bitcast.49, bf16[1,2048,64]{1,2,0:T(8,128)(2,1)S(1)} %bitcast.50, bf16[1,2048,64]{1,2,0:T(8,128)(2,1)S(1)} %bitcast.51, ...), kind=kOutput, calls=%fused_computation.10 | convolution fusion | flops 134643712 | bytes 3277316 | tf_op jit(solution)/shard_map/dot_general | solution.py:43
  51.8 0.0 copy-done.1
  51.8 1.4 %fusion.9 = f32[512,64]{0,1:T(8,128)} fusion(f32[512,64]{0,1:T(8,128)S(1)} %convolution_bitcast_fusion, f32[512,64]{0,1:T(8,128)S(1)} %fusion.15, bf16[2048,64]{0,1:T(8,128)(2,1)S(1)} %all_gather.3, bf16[1,2,512,2048]{3,2,1,0:T(8,128)(2,1)S(1)} %copy-done.1), kind=kOutput, calls=%fused_computation.8 | convolution fusion | flops 134283264 | bytes 2752512 | tf_op jit(solution)/shard_map/dot_general | solution.py:42
  (2 shorter events, 0.0 us)
Async XLA Ops:
  0.0 49.2 %copy-start = (bf16[512,64]{0,1:T(8,128)(2,1)S(1)}, bf16[512,64]{0,1:T(8,128)(2,1)}, u32[]{:S(2)}) copy-start(bf16[512,64]{0,1:T(8,128)(2,1)} %param.16) | copy-start | bytes 196612
  8.2 41.2 %collective-permute-start = (bf16[2048,64]{0,1:T(8,128)(2,1)S(1)}, bf16[2048,64]{0,1:T(8,128)(2,1)S(1)}, u32[]{:S(2)}, u32[]{:S(2)}) collective-permute-start(bf16[2048,64]{0,1:T(8,128)(2,1)S(1)} %all_gather.3), channel_id=1, source_target_pairs={{0,8},{4,12},{1,9},{5,13},{2,10},{6,14},{3,11},{7,15},{16,24},{20,... | collective-permute-start | bytes 786440 | tf_op jit(solution)/shard_map/ppermute | solution.py:16
  12.7 36.7 %collective-permute-start.1 = (bf16[2048,64]{0,1:T(8,128)(2,1)S(1)}, bf16[2048,64]{0,1:T(8,128)(2,1)S(1)}, u32[]{:S(2)}, u32[]{:S(2)}) collective-permute-start(bf16[2048,64]{0,1:T(8,128)(2,1)S(1)} %all_gather.3), channel_id=1, source_target_pairs={{0,4},{4,8},{8,12},{1,5},{5,9},{9,13},{2,6},{6,10},{10,14},{3,7},{... | collective-permute-start | bytes 786440 | tf_op jit(solution)/shard_map/ppermute | solution.py:16
  16.2 33.2 %collective-permute-start.2 = (bf16[2048,64]{0,1:T(8,128)(2,1)S(1)}, bf16[2048,64]{0,1:T(8,128)(2,1)S(1)}, u32[]{:S(2)}, u32[]{:S(2)}) collective-permute-start(bf16[2048,64]{0,1:T(8,128)(2,1)S(1)} %all_gather.3), channel_id=1, source_target_pairs={{4,0},{8,4},{12,8},{5,1},{9,5},{13,9},{6,2},{10,6},{14,10},{7,3},{... | collective-permute-start | bytes 786440 | tf_op jit(solution)/shard_map/ppermute | solution.py:16
  17.5 31.9 %collective-permute-start.3 = (bf16[2048,64]{0,1:T(8,128)(2,1)S(1)}, bf16[2048,64]{0,1:T(8,128)(2,1)S(1)}, u32[]{:S(2)}, u32[]{:S(2)}) collective-permute-start(bf16[2048,64]{0,1:T(8,128)(2,1)S(1)} %all_gather.3), channel_id=1, source_target_pairs={{8,0},{12,4},{9,1},{13,5},{10,2},{14,6},{11,3},{15,7},{24,16},{28,... | collective-permute-start | bytes 786440 | tf_op jit(solution)/shard_map/ppermute | solution.py:16
  32.0 13.6 %all-to-all-start = ((f32[4,1,4096]{2,1,0:T(1,128)}), f32[4,1,4096]{2,1,0:T(1,128)S(1)}, u32[]{:S(2)}, u32[]{:S(2)}) async-start(f32[4,1,4096]{2,1,0:T(1,128)} %reshape.65), calls=%async_computation | async-start | bytes 131072 | tf_op jit(solution)/shard_map/all_to_all | solution.py:9
  47.6 4.2 %copy-start.1 = (bf16[1,2,512,2048]{3,2,1,0:T(8,128)(2,1)S(1)}, bf16[1,2,512,2048]{3,2,1,0:T(8,128)(2,1)}, u32[]{:S(2)}) copy-start(bf16[1,2,512,2048]{3,2,1,0:T(8,128)(2,1)} %param.10) | copy-start | bytes 12582916
